TPU v7x, 32 devices: a whole 2x2x4 slice. The times are simulated.
32 devices in a mesh: row: 1, voc: 32 (over z, y, x, core).
Axes of the slice: x: 2, y: 2, z: 4, core: 2. Of those that a mesh axis runs over, the one named last changes fastest.
Arguments:
- hidden_states: bfloat16 [256, 4096], P('row'), may hold values from -72 to 72
- student_head: bfloat16 [4096, 65536], P('row', 'voc'), may hold values from -2 to 2
- teacher_probs: bfloat16 [256, 81920], P('row', 'voc'), may hold values from 9.9658966e-05 to 1
- block_map: int32 [512, 2], replicated, may hold values from 0 to 639, as said below
- context: int32 [4], P('row'), may hold values from 0 to 3
- map_gates: float32 [4, 512, 2], P(None, 'voc'), may hold values from 0.2 to 5
- map_tiles: bfloat16 [512, 2, 128, 128], P('voc'), may hold values from 0.0009994507 to 1
Outputs:
- grad_logits: bfloat16 [256, 65536], P('row', 'voc')
- head_grad: bfloat16 [4096, 65536], P('row', 'voc')
- kl_loss: float32 [], replicated
Inputs may be any that keep to these rules, and one draw needn't show every extreme that they name: `block_map`: in each aligned block of 16 student blocks, at most 2 of the 32 listed ids lie in any one aligned range of 20 teacher blocks, and exactly 2 in one such range.
All inputs are finite; a program needn't handle non-finite values.
Results may differ from a plain program's by a relative error of at most 0.013.
Values may be sent and summed in bfloat16 or wider, within the bound.
A program may use at most 128 MiB of HBM per device.

v0:
```python
import math
import jax
import jax.numpy as jnp
from jax import lax
from jax.sharding import PartitionSpec as P


def map_teacher(teacher_probs, block_map, context, map_gates, map_tiles):
    voc_count = lax.axis_size("voc")
    own_index = lax.axis_index("voc")
    blocks, fanout, block_width, _ = map_tiles.shape
    tokens_here = teacher_probs.shape[0]
    per_shard = teacher_probs.shape[1] // block_width
    entries = blocks * fanout
    capacity = entries // voc_count + 1
    wanted_all = block_map.reshape(voc_count, entries)
    sources_all = wanted_all // per_shard
    owned = (sources_all == own_index).astype(jnp.int32)
    rank_in = jnp.cumsum(owned, axis=1) - 1
    selected = owned[:, None, :] * (
        rank_in[:, None, :] == jnp.arange(capacity)[None, :, None]
    ).astype(jnp.int32)
    local_ids = wanted_all - own_index * per_shard
    take_index = jnp.sum(selected * local_ids[:, None, :], axis=2).reshape(-1)
    filled = jnp.sum(selected, axis=2).reshape(-1) > 0
    teacher_blocks = teacher_probs.reshape(tokens_here, per_shard, block_width)
    outgoing = jnp.where(
        filled[None, :, None],
        jnp.take(teacher_blocks, take_index, axis=1),
        jnp.zeros((), teacher_probs.dtype),
    )
    incoming = lax.all_to_all(outgoing, "voc", split_axis=1, concat_axis=1, tiled=True)
    wanted = lax.dynamic_index_in_dim(wanted_all, own_index, 0, keepdims=False)
    sources = wanted // per_shard
    source_hot = (sources[:, None] == jnp.arange(voc_count)[None, :]).astype(jnp.int32)
    position = jnp.sum(source_hot * (jnp.cumsum(source_hot, axis=0) - 1), axis=1)
    pieces = jnp.take(incoming, sources * capacity + position, axis=1).reshape(
        tokens_here, blocks, fanout, block_width
    )
    products = jnp.einsum("tbkj,bkjc->tbkc", pieces, map_tiles, preferred_element_type=jnp.float32)
    window = tokens_here // context.shape[0]
    token_context = jnp.repeat(context, window)
    context_count = map_gates.shape[0]
    context_hot = (token_context[:, None] == jnp.arange(context_count)[None, :]).astype(jnp.float32)
    gate_token = jnp.dot(
        context_hot, map_gates.reshape(context_count, entries), precision=lax.Precision.HIGHEST
    )
    gate_token = gate_token.reshape(tokens_here, blocks, fanout)
    mapped = jnp.sum(gate_token[..., None] * products, axis=2)
    return mapped.reshape(tokens_here, blocks * block_width)


def per_device(
    hidden_states, student_head, teacher_probs, block_map, context, map_gates, map_tiles
):
    tokens_here = hidden_states.shape[0]
    vocab_cols = student_head.shape[1]
    rows_total = tokens_here * lax.axis_size("row")
    inv_root = 1.0 / math.sqrt(rows_total)
    columns = hidden_states
    logits = jnp.dot(
        columns,
        lax.all_gather(student_head, "row", axis=0, tiled=True),
        preferred_element_type=jnp.float32,
    )
    mapped = map_teacher(teacher_probs, block_map, context, map_gates, map_tiles)
    local_total = jnp.sum(mapped, axis=1)
    peak = lax.pmax(jnp.max(logits, axis=1), "voc")
    summed, row_total = lax.psum(
        (jnp.sum(jnp.exp(logits - peak[:, None]), axis=1), local_total), "voc"
    )
    log_norm = peak + jnp.log(summed)
    target = mapped / row_total[:, None]
    vocab_total = vocab_cols * lax.axis_size("voc")
    grad_logits = (vocab_total * (jnp.exp(logits - log_norm[:, None]) - target)).astype(
        jnp.bfloat16
    )
    kl_partial = jnp.sum(target * (jnp.log(target) - logits + log_norm[:, None]))
    kl_loss = lax.psum(kl_partial, ("row", "voc")) / rows_total
    columns = hidden_states
    head_grad = lax.psum_scatter(
        (
            jnp.einsum("td,tv->dv", columns, grad_logits, preferred_element_type=jnp.float32)
            * inv_root
        ).astype(jnp.bfloat16),
        "row",
        scatter_dimension=0,
        tiled=True,
    )
    return (grad_logits, head_grad, kl_loss)


def solution(mesh):
    placed = (
        P("row", None),
        P("row", "voc"),
        P("row", "voc"),
        P(),
        P("row"),
        P(None, "voc", None),
        P("voc", None, None, None),
    )
    return jax.shard_map(
        per_device,
        mesh=mesh,
        in_specs=placed,
        out_specs=(P("row", "voc"), P("row", "voc"), P()),
        check_vma=False,
    )
```

profile of v0, /device:TPU:0, one launch (start us, length us, event | category | flops | bytes accessed | tf_op | source)
XLA Modules:
  0.0 265.5 jit_solution(6915176413589126362)
XLA Ops:
  0.6 1.0 copy.49
  1.8 0.2 reduce_window_sum.23
  2.7 2.4 copy.57
  5.2 1.8 copy.59
  6.9 3.1 %gather_fusion = bf16[64,256,128]{2,1,0:T(8,128)(2,1)} fusion(bf16[256,20,128]{2,0,1:T(8,128)(2,1)S(1)} %copy.59, s32[1024]{0:T(1024)S(1)} %pad_clamp_fusion.1), kind=kCustom, calls=%fused_computation | custom fusion | bytes 8388864 | tf_op jit(solution)/shard_map/jit(_take)/gather | solution.py:29
  10.0 4.0 %select_bitcast_fusion = bf16[256,64,128]{2,0,1:T(8,128)(2,1)} fusion(bf16[64,256,128]{2,1,0:T(8,128)(2,1)} %gather_fusion, pred[64]{0:T(512)(128)(4,1)S(1)} %gt.19, pred[64]{0:T(512)(128)(4,1)S(1)} %compare_and_fusion), kind=kLoop, calls=%fused_computation.5 | loop fusion | flops 4194304 | bytes 8388736 | tf_op jit(solution)/shard_map/jit(_where)/select_n | solution.py:27
  14.0 7.4 %all-to-all-start = ((bf16[256,64,128]{2,0,1:T(8,128)(2,1)}), bf16[256,64,128]{2,0,1:T(8,128)(2,1)}, u32[]{:S(2)}, u32[]{:S(2)}) async-start(bf16[256,64,128]{2,0,1:T(8,128)(2,1)} %select_bitcast_fusion), calls=%async_computation | async-start | bytes 8388608 | tf_op jit(solution)/shard_map/all_to_all | solution.py:32
  21.6 0.2 fusion.12
  21.9 0.5 broadcast.277
  22.4 0.7 fusion.25
  23.3 0.5 broadcast.278
  23.8 0.7 fusion.24
  24.8 0.2 select_reduce_fusion.1
  25.3 9.6 %fusion.26 = (f32[256]{0:T(256)S(1)}, f32[256,2048]{1,0:T(8,128)}) fusion(bf16[256,4096]{1,0:T(8,128)(2,1)S(1)} %copy-done, bf16[4096,2048]{1,0:T(8,128)(2,1)} %param.8), kind=kOutput, calls=%fused_computation.61 | convolution fusion | flops 4295491584 | bytes 20972544 | tf_op jit(solution)/shard_map/dot_general | solution.py:61
  34.9 100.9 %pmax.7 = f32[256]{0:T(256)S(1)} all-reduce(f32[256]{0:T(256)S(1)} %get-tuple-element.30), channel_id=1, replica_groups=mesh['row'=1,'voc'=32] {'voc'}, use_global_device_ids=true, to_apply=%region_1.2 | all-reduce | flops 256 | bytes 2048 | tf_op jit(solution)/shard_map/pmax | solution.py:68
  135.8 2.0 exponential_reduce_fusion
  137.8 4.4 %gather_fusion.1 = bf16[32,256,128]{2,1,0:T(8,128)(2,1)} fusion(bf16[256,64,128]{2,0,1:T(8,128)(2,1)} %all-to-all-done, s32[1024]{0:T(1024)S(1)} %pad_clamp_fusion), kind=kCustom, calls=%fused_computation.1 | custom fusion | bytes 4194432 | tf_op jit(solution)/shard_map/jit(_take)/gather | solution.py:37
  142.2 4.0 %fusion.1 = (f32[256]{0:T(256)S(1)}, f32[256,16,128]{0,2,1:T(8,128)}) fusion(f32[256,16,2]{0,2,1:T(2,128)S(1)} %copy.48, bf16[16,2,128,128]{3,2,1,0:T(8,128)(2,1)S(1)} %copy-done.3, bf16[256,16,2,128]{3,0,2,1:T(8,128)(2,1)} %bitcast.52, pred[16,2]{1,0:T(8,128)(4,1)S(1)} %copy.54), kind=kOutput, calls=%fused_computation.6 | convolution fusion | flops 272105216 | bytes 5276704 | tf_op jit(solution)/shard_map/tbkj,bkjc->tbkc/dot_general | solution.py:40
  146.2 2.9 %copy.65 = f32[256,2048]{1,0:T(8,128)} copy(f32[256,2048]{0,1:T(8,128)} %bitcast.53) | data formatting | bytes 4194304 | tf_op jit(solution)/shard_map/reshape | solution.py:50
  149.1 38.1 %all-reduce = (f32[256]{0:T(256)S(1)}, f32[256]{0:T(256)S(1)}) all-reduce(f32[256]{0:T(256)S(1)} %exponential_reduce_fusion, f32[256]{0:T(256)S(1)} %get-tuple-element.18), channel_id=1, replica_groups=mesh['row'=1,'voc'=32] {'voc'}, use_global_device_ids=true, to_apply=%region_3.4 | all-reduce | flops 512 | bytes 4096 | tf_op jit(solution)/shard_map/psum | solution.py:69
  187.2 3.8 %multiply_reduce_fusion = (f32[]{:T(128)}, bf16[256,2048]{1,0:T(8,128)(2,1)S(1)}) fusion(f32[256,2048]{1,0:T(8,128)} %get-tuple-element.31, f32[256]{0:T(256)S(1)} %log_add_fusion, f32[256,2048]{1,0:T(8,128)} %copy.65, f32[256]{0:T(256)S(1)} %get-tuple-element.23), kind=kLoop, calls=%fused_computation.8 | loop fusion | flops 4718591 | bytes 5244932 | tf_op jit(solution)/shard_map/reduce_sum | solution.py:78
  191.0 42.2 %psum.23 = f32[]{:T(128)} all-reduce(f32[]{:T(128)} %get-tuple-element.28), channel_id=1, replica_groups=mesh['row'=1,'voc'=32] {'row','voc'}, use_global_device_ids=true, to_apply=%region_13.14 | all-reduce | flops 1 | bytes 8 | tf_op jit(solution)/shard_map/psum | solution.py:79
  233.3 8.1 %fusion = bf16[4096,2048]{0,1:T(8,128)(2,1)} fusion(bf16[256,2048]{1,0:T(8,128)(2,1)S(1)} %get-tuple-element.29, bf16[256,4096]{1,0:T(8,128)(2,1)S(1)} %copy-done), kind=kOutput, calls=%fused_computation.3 | convolution fusion | flops 4311744512 | bytes 19922944 | tf_op jit(solution)/shard_map/td,tv->dv/dot_general | solution.py:83
  241.3 22.4 %copy.62 = bf16[4096,2048]{1,0:T(8,128)(2,1)} copy(bf16[4096,2048]{0,1:T(8,128)(2,1)} %fusion) | data formatting | bytes 33554432
  (41 shorter events, 1.9 us)
Async XLA Ops:
  0.6 24.6 %copy-start = (bf16[256,4096]{1,0:T(8,128)(2,1)S(1)}, bf16[256,4096]{1,0:T(8,128)(2,1)}, u32[]{:S(2)}) copy-start(bf16[256,4096]{1,0:T(8,128)(2,1)} %param.7) | copy-start | bytes 6291460
  14.0 7.4 %copy-start.2 = (s32[4]{0:T(128)S(1)}, s32[4]{0:T(128)}, u32[]{:S(2)}) copy-start(s32[4]{0:T(128)} %param.11) | copy-start | bytes 52
  14.0 7.6 %copy-start.4 = (f32[4,16,2]{1,2,0:T(2,128)S(1)}, f32[4,16,2]{1,2,0:T(2,128)}, u32[]{:S(2)}) copy-start(f32[4,16,2]{1,2,0:T(2,128)} %param.12) | copy-start | bytes 1540
  14.0 123.8 %all-to-all-start = ((bf16[256,64,128]{2,0,1:T(8,128)(2,1)}), bf16[256,64,128]{2,0,1:T(8,128)(2,1)}, u32[]{:S(2)}, u32[]{:S(2)}) async-start(bf16[256,64,128]{2,0,1:T(8,128)(2,1)} %select_bitcast_fusion), calls=%async_computation | async-start | bytes 8388608 | tf_op jit(solution)/shard_map/all_to_all | solution.py:32
  137.8 4.4 %copy-start.3 = (bf16[16,2,128,128]{3,2,1,0:T(8,128)(2,1)S(1)}, bf16[16,2,128,128]{3,2,1,0:T(8,128)(2,1)}, u32[]{:S(2)}) copy-start(bf16[16,2,128,128]{3,2,1,0:T(8,128)(2,1)} %param.13) | copy-start | bytes 3145732
  191.0 50.3 %copy-start.1 = (bf16[256,2048]{1,0:T(8,128)(2,1)}, bf16[256,2048]{1,0:T(8,128)(2,1)S(1)}, u32[]{:S(2)}) copy-start(bf16[256,2048]{1,0:T(8,128)(2,1)S(1)} %get-tuple-element.29) | copy-start | bytes 3145732
where the time goes:
time: 267 us; the launch traced here: 266 us
  blocking collectives  181 us (68%)
  local copies, waits for them, and re-layouts  40.5 us (15%)
  matrix products  21.9 us (8%)
  other arithmetic  12 us (4%)
  starting transfers between devices  7.43 us (3%)
    pmax x1, blocking collectives, per_device(): peak = lax.pmax(jnp.max(logits, axis=1), 'voc')  101 us
    psum x1, blocking collectives, per_device(): kl_loss = lax.psum(kl_partial, ('row', 'voc')) / rows_total  42.2 us
    psum x1, blocking collectives, per_device(): lax.psum((jnp.sum(jnp.exp(logits - peak[:, None]), axis=1), local_total),...  38.1 us
    unnamed x13, local copies, waits for them, and re-layouts  25.9 us
    dot_general x1, matrix products, per_device(): jnp.dot(columns, lax.all_gather(student_head, 'row', axis=0, tiled=True),...  9.62 us
    dot_general x1, matrix products, per_device(): jnp.einsum('td,tv->dv', columns, grad_logits, preferred_element_type=jnp....  8.08 us
    all_to_all x1, starting transfers between devices, map_teacher(): lax.all_to_all(outgoing, 'voc', split_axis=1, concat_axis=1, tiled=True)  7.43 us
  transfers between devices with their start and end apart: 1, of which 0 were waited for; matrix products, arithmetic and copies ran while one was open for 6% of the time, Pallas kernels for 0%

commit v1 on v0

--- a/solution.py
+++ b/solution.py
@@ -29,7 +29,9 @@
         jnp.take(teacher_blocks, take_index, axis=1),
         jnp.zeros((), teacher_probs.dtype),
     )
-    incoming = lax.all_to_all(outgoing, "voc", split_axis=1, concat_axis=1, tiled=True)
+    shards = jnp.split(outgoing, lax.axis_size("voc"), axis=1)
+    incoming_2 = lax.all_to_all(jnp.stack(shards), "voc", 0, 0)
+    incoming = jnp.concatenate(incoming_2, axis=1)
     wanted = lax.dynamic_index_in_dim(wanted_all, own_index, 0, keepdims=False)
     sources = wanted // per_shard
     source_hot = (sources[:, None] == jnp.arange(voc_count)[None, :]).astype(jnp.int32)

time: 267 us -> 286 us (1.071)
  local copies, waits for them, and re-layouts: 40.5 us -> 61.7 us
    unnamed x13 -> x44, local copies, waits for them, and re-layouts: 25.9 us -> 46.4 us
  transfers between devices with their start and end apart: 1 -> 1, of which waited for: 0 -> 0; matrix products, arithmetic and copies ran while one was open for 6% -> 5% of each run, Pallas kernels for 0% -> 0%
where the time goes in v1:
time: 286 us; the launch traced here: 285 us
  blocking collectives  181 us (63%)
  local copies, waits for them, and re-layouts  61.7 us (22%)
  matrix products  21.9 us (8%)
  other arithmetic  10.6 us (4%)
  starting transfers between devices  7.43 us (3%)
    pmax x1, blocking collectives, per_device(): peak = lax.pmax(jnp.max(logits, axis=1), 'voc')  101 us
    unnamed x44, local copies, waits for them, and re-layouts  46.4 us
    psum x1, blocking collectives, per_device(): kl_loss = lax.psum(kl_partial, ('row', 'voc')) / rows_total  42.2 us
    psum x1, blocking collectives, per_device(): lax.psum((jnp.sum(jnp.exp(logits - peak[:, None]), axis=1), local_total),...  38.1 us
    dot_general x1, matrix products, per_device(): jnp.dot(columns, lax.all_gather(student_head, 'row', axis=0, tiled=True),...  9.62 us
    dot_general x1, matrix products, per_device(): jnp.einsum('td,tv->dv', columns, grad_logits, preferred_element_type=jnp....  8.08 us
    all_to_all x1, starting transfers between devices, map_teacher(): incoming_2 = lax.all_to_all(jnp.stack(shards), 'voc', 0, 0)  7.43 us
  transfers between devices with their start and end apart: 1, of which 0 were waited for; matrix products, arithmetic and copies ran while one was open for 5% of the time, Pallas kernels for 0%

profile of v1, /device:TPU:0, one launch (start us, length us, event | category | flops | bytes accessed | tf_op | source)
XLA Modules:
  0.0 285.4 jit_solution(7378014420723336388)
XLA Ops:
  0.6 1.0 copy.48
  2.7 2.4 copy.56
  5.2 1.8 copy.58
  6.9 3.1 %gather_fusion = bf16[64,256,128]{2,1,0:T(8,128)(2,1)} fusion(bf16[256,20,128]{2,0,1:T(8,128)(2,1)S(1)} %copy.58, s32[1024]{0:T(1024)S(1)} %pad_clamp_fusion.1), kind=kCustom, calls=%fused_computation | custom fusion | bytes 8388864 | tf_op jit(solution)/shard_map/jit(_take)/gather | solution.py:29
  10.0 2.7 select_bitcast_fusion
  12.7 0.7 fusion.38
  16.0 0.7 fusion.33
  17.3 0.7 fusion.31
  18.7 0.7 fusion.29
  20.0 0.7 fusion.27
  34.0 7.4 %all-to-all-start = ((bf16[32,256,2,128]{3,1,2,0:T(8,128)(2,1)}), bf16[32,256,2,128]{3,1,2,0:T(8,128)(2,1)}, u32[]{:S(2)}, u32[]{:S(2)}) async-start(bf16[32,256,2,128]{3,1,2,0:T(8,128)(2,1)} %fusion.7), calls=%async_computation | async-start | bytes 8388608 | tf_op jit(solution)/shard_map/all_to_all | solution.py:33
  42.3 0.7 fusion.57
  43.7 0.7 fusion.56
  45.2 9.6 %fusion.58 = (f32[256]{0:T(256)S(1)}, f32[256,2048]{1,0:T(8,128)}) fusion(bf16[256,4096]{1,0:T(8,128)(2,1)S(1)} %copy-done, bf16[4096,2048]{1,0:T(8,128)(2,1)} %param.8), kind=kOutput, calls=%fused_computation.125 | convolution fusion | flops 4295491584 | bytes 20972544 | tf_op jit(solution)/shard_map/dot_general | solution.py:63
  54.8 100.9 %pmax.7 = f32[256]{0:T(256)S(1)} all-reduce(f32[256]{0:T(256)S(1)} %get-tuple-element.30), channel_id=1, replica_groups=mesh['row'=1,'voc'=32] {'voc'}, use_global_device_ids=true, to_apply=%region_1.2 | all-reduce | flops 256 | bytes 2048 | tf_op jit(solution)/shard_map/pmax | solution.py:70
  155.7 2.0 exponential_reduce_fusion
  157.7 4.3 %gather_fusion.1 = bf16[32,256,128]{2,1,0:T(8,128)(2,1)} fusion(bf16[256,64,128]{2,0,1:T(8,128)(2,1)} %bitcast.43, s32[1024]{0:T(1024)S(1)} %pad_clamp_fusion), kind=kCustom, calls=%fused_computation.1 | custom fusion | bytes 4194432 | tf_op jit(solution)/shard_map/jit(_take)/gather | solution.py:39
  162.0 4.0 %fusion.1 = (f32[256]{0:T(256)S(1)}, f32[256,16,128]{0,2,1:T(8,128)}) fusion(f32[256,16,2]{0,2,1:T(2,128)S(1)} %copy.47, bf16[16,2,128,128]{3,2,1,0:T(8,128)(2,1)S(1)} %copy-done.3, bf16[256,16,2,128]{3,0,2,1:T(8,128)(2,1)} %bitcast.183, pred[16,2]{1,0:T(8,128)(4,1)S(1)} %copy.53), kind=kOutput, calls=%fused_computation.6 | convolution fusion | flops 272105216 | bytes 5276704 | tf_op jit(solution)/shard_map/tbkj,bkjc->tbkc/dot_general | solution.py:42
  166.0 2.9 %copy.64 = f32[256,2048]{1,0:T(8,128)} copy(f32[256,2048]{0,1:T(8,128)} %bitcast.184) | data formatting | bytes 4194304 | tf_op jit(solution)/shard_map/reshape | solution.py:52
  168.9 38.1 %all-reduce = (f32[256]{0:T(256)S(1)}, f32[256]{0:T(256)S(1)}) all-reduce(f32[256]{0:T(256)S(1)} %exponential_reduce_fusion, f32[256]{0:T(256)S(1)} %get-tuple-element.18), channel_id=1, replica_groups=mesh['row'=1,'voc'=32] {'voc'}, use_global_device_ids=true, to_apply=%region_3.4 | all-reduce | flops 512 | bytes 4096 | tf_op jit(solution)/shard_map/psum | solution.py:71
  207.0 3.8 %multiply_reduce_fusion = (f32[]{:T(128)}, bf16[256,2048]{1,0:T(8,128)(2,1)S(1)}) fusion(f32[256,2048]{1,0:T(8,128)} %get-tuple-element.31, f32[256]{0:T(256)S(1)} %log_add_fusion, f32[256,2048]{1,0:T(8,128)} %copy.64, f32[256]{0:T(256)S(1)} %get-tuple-element.23), kind=kLoop, calls=%fused_computation.8 | loop fusion | flops 4718591 | bytes 5244932 | tf_op jit(solution)/shard_map/reduce_sum | solution.py:80
  210.9 42.2 %psum.23 = f32[]{:T(128)} all-reduce(f32[]{:T(128)} %get-tuple-element.28), channel_id=1, replica_groups=mesh['row'=1,'voc'=32] {'row','voc'}, use_global_device_ids=true, to_apply=%region_13.14 | all-reduce | flops 1 | bytes 8 | tf_op jit(solution)/shard_map/psum | solution.py:81
  253.1 8.1 %fusion = bf16[4096,2048]{0,1:T(8,128)(2,1)} fusion(bf16[256,2048]{1,0:T(8,128)(2,1)S(1)} %get-tuple-element.29, bf16[256,4096]{1,0:T(8,128)(2,1)S(1)} %copy-done), kind=kOutput, calls=%fused_computation.3 | convolution fusion | flops 4311744512 | bytes 19922944 | tf_op jit(solution)/shard_map/td,tv->dv/dot_general | solution.py:85
  261.1 22.4 %copy.61 = bf16[4096,2048]{1,0:T(8,128)(2,1)} copy(bf16[4096,2048]{0,1:T(8,128)(2,1)} %fusion) | data formatting | bytes 33554432
  (73 shorter events, 21.4 us)
Async XLA Ops:
  0.6 44.6 %copy-start = (bf16[256,4096]{1,0:T(8,128)(2,1)S(1)}, bf16[256,4096]{1,0:T(8,128)(2,1)}, u32[]{:S(2)}) copy-start(bf16[256,4096]{1,0:T(8,128)(2,1)} %param.7) | copy-start | bytes 6291460
  34.0 7.4 %copy-start.2 = (s32[4]{0:T(128)S(1)}, s32[4]{0:T(128)}, u32[]{:S(2)}) copy-start(s32[4]{0:T(128)} %param.11) | copy-start | bytes 52
  34.0 7.6 %copy-start.4 = (f32[4,16,2]{1,2,0:T(2,128)S(1)}, f32[4,16,2]{1,2,0:T(2,128)}, u32[]{:S(2)}) copy-start(f32[4,16,2]{1,2,0:T(2,128)} %param.12) | copy-start | bytes 1540
  34.0 123.7 %all-to-all-start = ((bf16[32,256,2,128]{3,1,2,0:T(8,128)(2,1)}), bf16[32,256,2,128]{3,1,2,0:T(8,128)(2,1)}, u32[]{:S(2)}, u32[]{:S(2)}) async-start(bf16[32,256,2,128]{3,1,2,0:T(8,128)(2,1)} %fusion.7), calls=%async_computation | async-start | bytes 8388608 | tf_op jit(solution)/shard_map/all_to_all | solution.py:33
  54.8 107.2 %copy-start.3 = (bf16[16,2,128,128]{3,2,1,0:T(8,128)(2,1)S(1)}, bf16[16,2,128,128]{3,2,1,0:T(8,128)(2,1)}, u32[]{:S(2)}) copy-start(bf16[16,2,128,128]{3,2,1,0:T(8,128)(2,1)} %param.13) | copy-start | bytes 3145732
  210.9 50.3 %copy-start.1 = (bf16[256,2048]{1,0:T(8,128)(2,1)}, bf16[256,2048]{1,0:T(8,128)(2,1)S(1)}, u32[]{:S(2)}) copy-start(bf16[256,2048]{1,0:T(8,128)(2,1)S(1)} %get-tuple-element.29) | copy-start | bytes 3145732
